TPU v7x, 32 devices: a whole 2x2x4 slice. The times are simulated.
32 devices in a mesh: tm: 2 (over y), rows: 4 (over z), dp: 4 (over x, core).
Axes of the slice: x: 2, y: 2, z: 4, core: 2. Of those that a mesh axis runs over, the one named last changes fastest.
Arguments:
- video: bfloat16 [4, 32, 16, 32, 128], P('dp', 'tm', 'rows'), may hold values from -6 to 6
- cotangent: bfloat16 [4, 32, 16, 32, 128], P('dp', 'tm', 'rows'), may hold values from -6 to 6
- in_kernel: bfloat16 [3, 3, 128, 128], replicated, may hold values from -0.03125 to 0.03125
- out_kernel: bfloat16 [3, 3, 128, 128], replicated, may hold values from -0.1875 to 0.1875
- skip_gain: float32 [128], replicated, may hold values from 0.5 to 1.5
- log_decay: float32 [32, 128], P('tm'), may hold values from -3 to 0, as said below
Outputs:
- layer_out: bfloat16 [4, 32, 16, 32, 128], P('dp', 'tm', 'rows')
- video_grad: bfloat16 [4, 32, 16, 32, 128], P('dp', 'tm', 'rows')
- in_kernel_grad: float32 [3, 3, 128, 128], replicated
- out_kernel_grad: float32 [3, 3, 128, 128], replicated
- skip_gain_grad: float32 [128], replicated
- decay_grad: float32 [32, 128], P('tm')
Inputs may be any that keep to these rules, and one draw needn't show every extreme that they name: log_decay is negative.
All inputs are finite; a program needn't handle non-finite values.
Results may differ from a plain program's by a relative error of at most 0.0085.
Values may be sent and summed in bfloat16 or wider, within the bound.
No kernel may reach another device: no remote copies, remote signals or barrier semaphores. Data moves between devices by JAX's collectives and lax.ppermute only.
A program may use at most 64 MiB of HBM per device.

v0:
```python
import math
import jax
import jax.numpy as jnp
from jax import lax
from jax.sharding import PartitionSpec as P


def padded_2(cells, sides, width):
    for axis, dim in sides:
        count = lax.axis_size(axis)
        ends = count - 1
        head = lax.slice_in_dim(cells, 0, width, axis=dim)
        tail = lax.slice_in_dim(cells, cells.shape[dim] - width, cells.shape[dim], axis=dim)
        cells = jnp.concatenate(
            [
                lax.ppermute(tail, axis, [(i, (i + 1) % count) for i in range(ends)]),
                cells,
                lax.ppermute(head, axis, [((i + 1) % count, i) for i in range(ends)]),
            ],
            axis=dim,
        )
    return cells


def pad_columns(field):
    return jnp.pad(field, ((0, 0), (0, 0), (0, 0), (1, 1), (0, 0)))


def forward_conv(padded, kernel):
    seqs, frames, rows_two, cols_two, chans = padded.shape
    rows, cols = (rows_two - 2, cols_two - 2)
    total = None
    for i in range(3):
        for j in range(3):
            piece = padded[:, :, i : i + rows, j : j + cols, :].reshape(-1, chans)
            term = jnp.dot(piece, kernel[i, j], preferred_element_type=jnp.float32)
            total = term if total is None else total + term
    return total.reshape(seqs, frames, rows, cols, kernel.shape[3])


def adjoint_conv(padded, kernel):
    seqs, frames, rows_two, cols_two, chans = padded.shape
    rows, cols = (rows_two - 2, cols_two - 2)
    total = None
    for i in range(3):
        for j in range(3):
            piece = padded[:, :, 2 - i : 2 - i + rows, 2 - j : 2 - j + cols, :].reshape(-1, chans)
            term = lax.dot_general(
                piece, kernel[i, j], (((1,), (1,)), ((), ())), preferred_element_type=jnp.float32
            )
            total = term if total is None else total + term
    return total.reshape(seqs, frames, rows, cols, kernel.shape[2])


def kernel_grad(padded, grad):
    seqs, frames, rows_two, cols_two, chans = padded.shape
    rows, cols = (rows_two - 2, cols_two - 2)
    flat_grad = grad.reshape(-1, grad.shape[-1])
    outer_list = []
    for i in range(3):
        inner_list = []
        for j in range(3):
            piece = padded[:, :, i : i + rows, j : j + cols, :].reshape(-1, chans)
            inner_list.append(
                lax.dot_general(
                    piece, flat_grad, (((0,), (0,)), ((), ())), preferred_element_type=jnp.float32
                )
            )
        outer_list.append(jnp.stack(inner_list))
    return jnp.stack(outer_list)


def on_device(video, cotangent, in_kernel, out_kernel, skip_gain, log_decay):
    seqs, frames, rows, cols, chans = video.shape
    padded_x = pad_columns(padded_2(video, (("rows", 2),), 1))
    drive = forward_conv(padded_x, in_kernel)
    cum = jnp.cumsum(log_decay, axis=0)
    later_mask = (
        lax.broadcasted_iota(jnp.int32, (frames, frames), 0)
        >= lax.broadcasted_iota(jnp.int32, (frames, frames), 1)
    )[:, :, None]
    gaps = cum[:, None, :] - cum[None, :, :]
    within = jnp.where(later_mask, jnp.exp(jnp.where(later_mask, gaps, 0.0)), 0.0)
    local_states = jnp.einsum("tkp,skrcp->strcp", within, drive, precision=lax.Precision.HIGHEST)
    group_total = cum[-1]
    empty = jnp.zeros_like(local_states[:, -1])
    group_logs = lax.all_gather(group_total[None, :], "tm", axis=0, tiled=True)
    running = jnp.cumsum(group_logs, axis=0)
    own = lax.axis_index("tm")
    own_running = lax.dynamic_index_in_dim(running, own, 0, keepdims=False)
    piece = lax.all_gather(
        local_states[:, -1][None].astype(jnp.bfloat16), "tm", axis=0, tiled=True
    ).astype(jnp.float32)
    count = piece.shape[0]
    upto = running
    index = jnp.arange(count, dtype=jnp.int32)
    reach = own_running[None, :] - group_total[None, :] - upto
    weight = jnp.where((index < own)[:, None], jnp.exp(jnp.minimum(reach, 0.0)), 0.0)
    carry_in = empty + jnp.einsum("np,nsrcp->srcp", weight, piece, precision=lax.Precision.HIGHEST)
    states = local_states + jnp.exp(cum)[None, :, None, None, :] * carry_in[:, None]
    states_bf = states.astype(jnp.bfloat16)
    padded_s = pad_columns(padded_2(states_bf, (("rows", 2),), 1))
    pre = forward_conv(padded_s, out_kernel) + skip_gain * video.astype(jnp.float32)
    activated, pullback = jax.vjp(jax.nn.gelu, pre)
    grad_pre = pullback(cotangent.astype(jnp.float32))[0]
    grad_bf = grad_pre.astype(jnp.bfloat16)
    out_grad = kernel_grad(padded_s, grad_bf)
    gain_grad = jnp.sum(grad_pre * video.astype(jnp.float32), axis=(0, 1, 2, 3))
    padded_g = pad_columns(padded_2(grad_bf, (("rows", 2),), 1))
    state_grad = adjoint_conv(padded_g, out_kernel)
    local_adjoint = jnp.einsum(
        "tkp,strcp->skrcp", within, state_grad, precision=lax.Precision.HIGHEST
    )
    leading = jnp.exp(cum[0])[None, None, None, :] * local_adjoint[:, 0]
    piece = lax.all_gather(leading[None].astype(jnp.bfloat16), "tm", axis=0, tiled=True).astype(
        jnp.float32
    )
    count = piece.shape[0]
    upto = running
    index = jnp.arange(count, dtype=jnp.int32)
    reach = upto - group_logs - own_running[None, :]
    weight = jnp.where((index > own)[:, None], jnp.exp(jnp.minimum(reach, 0.0)), 0.0)
    back_in = empty + jnp.einsum("np,nsrcp->srcp", weight, piece, precision=lax.Precision.HIGHEST)
    adjoint = (
        local_adjoint
        + jnp.exp(group_total[None, :] - cum)[None, :, None, None, :] * back_in[:, None]
    )
    previous = jnp.concatenate([carry_in[:, None], states[:, :-1]], axis=1)
    decay_part = jnp.sum(
        adjoint * jnp.exp(log_decay)[None, :, None, None, :] * previous, axis=(0, 2, 3)
    )
    decay_scale = 1.0 / math.sqrt(seqs * rows * cols * lax.axis_size("rows") * lax.axis_size("dp"))
    decay_grad = lax.psum(decay_part, ("rows", "dp")) * decay_scale
    adjoint_bf = adjoint.astype(jnp.bfloat16)
    in_grad = kernel_grad(padded_x, adjoint_bf)
    padded_a = pad_columns(padded_2(adjoint_bf, (("rows", 2),), 1))
    video_grad = (adjoint_conv(padded_a, in_kernel) + skip_gain * grad_pre).astype(jnp.bfloat16)
    in_sum, out_sum, gain_sum = lax.psum((in_grad, out_grad, gain_grad), ("tm", "rows", "dp"))
    weight_scale = 1.0 / math.sqrt(
        seqs
        * frames
        * rows
        * cols
        * lax.axis_size("tm")
        * lax.axis_size("rows")
        * lax.axis_size("dp")
    )
    return (
        activated.astype(jnp.bfloat16),
        video_grad,
        in_sum * weight_scale,
        out_sum * weight_scale,
        gain_sum * weight_scale,
        decay_grad,
    )


def solution(mesh):
    placed = (
        P("dp", "tm", "rows", None, None),
        P("dp", "tm", "rows", None, None),
        P(),
        P(),
        P(),
        P("tm", None),
    )
    return jax.shard_map(
        on_device,
        mesh=mesh,
        in_specs=placed,
        out_specs=(
            P("dp", "tm", "rows", None, None),
            P("dp", "tm", "rows", None, None),
            P(),
            P(),
            P(),
            P("tm", None),
        ),
        check_vma=False,
    )
```

profile of v0, /device:TPU:0, one launch (start us, length us, event | category | flops | bytes accessed | tf_op | source)
XLA Modules:
  0.0 367.8 jit_solution(14901978521855251328)
XLA Ops:
  7.2 1.0 fusion.177
  8.2 5.0 %collective-permute-start = (bf16[1,16,1,32,128]{4,3,2,1,0:T(8,128)(2,1)S(1)}, bf16[1,16,1,32,128]{4,3,2,1,0:T(8,128)(2,1)S(1)}, u32[]{:S(2)}, u32[]{:S(2)}) collective-permute-start(bf16[1,16,1,32,128]{4,3,2,1,0:T(8,128)(2,1)S(1)} %get-tuple-element.71), channel_id=1, source_target_pairs={{0,4},{4,8},{8,12},{1,5},{5,9},{9,13},{2,6},{6,10},{10,14},{3,7},{... | collective-permute-start | bytes 393224 | tf_op jit(solution)/shard_map/ppermute | solution.py:16
  13.2 1.3 collective-permute-start.1
  15.2 4.2 %all-gather = f32[2,1,128]{2,1,0:T(1,128)S(1)} all-gather(f32[1,1,128]{2,1,0:T(1,128)S(1)} %slice_bitcast_fusion.1), channel_id=1, replica_groups=mesh['tm'=2,'rows'=4,'dp'=4] {'tm'}, dimensions={0}, use_global_device_ids=true | all-gather | bytes 1536 | tf_op jit(solution)/shard_map/all_gather | solution.py:87
  20.0 1.6 fusion.25
  25.6 4.5 %copy.169 = f32[16,4,32,128]{2,0,1,3:T(8,128)} copy(f32[16,4,32,128]{3,2,1,0:T(8,128)S(1)} %bitcast.443) | data formatting | bytes 2097152 | tf_op jit(solution)/shard_map/reshape
  30.1 8.3 %fusion.19 = f32[128,4,32,16]{2,3,1,0:T(8,128)} fusion(f32[16,4,32,128]{2,0,1,3:T(8,128)} %copy.169, f32[16,128]{0,1:T(8,128)S(1)} %copy.167, pred[16,16]{0,1:T(8,128)(4,1)S(1)} %iota_compare_fusion.2), kind=kOutput, calls=%fused_computation.74 | convolution fusion | flops 50429952 | bytes 2105600 | tf_op jit(solution)/shard_map/tkp,skrcp->strcp/dot_general | solution.py:84
  38.4 3.7 %copy.171 = f32[128,4,32,16]{0,2,1,3:T(8,128)S(1)} copy(f32[128,4,32,16]{2,3,1,0:T(8,128)} %fusion.19) | data formatting | bytes 2097152 | tf_op jit(solution)/shard_map/tkp,skrcp->strcp/dot_general | solution.py:84
  42.1 4.6 %all_gather.9 = bf16[2,1,4,32,128]{4,3,2,1,0:T(8,128)(2,1)S(1)} all-gather(bf16[1,1,4,32,128]{4,3,2,1,0:T(8,128)(2,1)S(1)} %slice.550), channel_id=1, replica_groups=mesh['tm'=2,'rows'=4,'dp'=4] {'tm'}, dimensions={0}, use_global_device_ids=true | all-gather | bytes 98304 | tf_op jit(solution)/shard_map/all_gather | solution.py:91
  47.0 4.2 %collective-permute-start.2 = (bf16[1,16,1,32,128]{4,3,2,1,0:T(8,128)(2,1)S(1)}, bf16[1,16,1,32,128]{4,3,2,1,0:T(8,128)(2,1)S(1)}, u32[]{:S(2)}, u32[]{:S(2)}) collective-permute-start(bf16[1,16,1,32,128]{4,3,2,1,0:T(8,128)(2,1)S(1)} %get-tuple-element.67), channel_id=1, source_target_pairs={{0,4},{4,8},{8,12},{1,5},{5,9},{9,13},{2,6},{6,10},{10,14},{3,7},{... | collective-permute-start | bytes 393224 | tf_op jit(solution)/shard_map/ppermute | solution.py:16
  51.2 1.5 collective-permute-start.3
  52.7 1.1 slice.347
  53.9 4.2 %collective-permute-done.3 = bf16[1,16,1,32,128]{4,3,2,1,0:T(8,128)(2,1)S(1)} collective-permute-done((bf16[1,16,1,32,128]{4,3,2,1,0:T(8,128)(2,1)S(1)}, bf16[1,16,1,32,128]{4,3,2,1,0:T(8,128)(2,1)S(1)}, u32[]{:S(2)}, u32[]{:S(2)}) %collective-permute-start.3) | collective-permute-done | bytes 131104 | tf_op jit(solution)/shard_map/ppermute | solution.py:18
  62.9 1.8 fusion.6
  64.8 1.0 convolution_bitcast_fusion.4
  65.8 1.0 convolution_bitcast_fusion.1
  66.7 1.0 convolution_bitcast_fusion.7
  67.7 1.0 convolution_bitcast_fusion.5
  68.7 1.0 convolution_bitcast_fusion.3
  69.7 1.0 convolution_bitcast_fusion.2
  70.6 1.0 convolution_bitcast_fusion
  71.6 1.0 convolution_bitcast_fusion.8
  72.5 1.0 convolution_bitcast_fusion.6
  74.2 40.4 %psum.30 = f32[128]{0:T(128)S(1)} all-reduce(f32[128]{0:T(128)S(1)} %get-tuple-element.26), channel_id=1, replica_groups=mesh['tm'=2,'rows'=4,'dp'=4] {'tm','rows','dp'}, use_global_device_ids=true, to_apply=%region_5.6 | all-reduce | flops 128 | bytes 1024 | tf_op jit(solution)/shard_map/psum | solution.py:138
  115.1 2.2 collective-permute-start.4
  117.3 1.5 collective-permute-start.5
  118.8 0.9 maximum_bitcast_fusion.4
  119.7 0.9 maximum_bitcast_fusion.5
  122.4 1.9 collective-permute-done.5
  127.9 1.3 fusion.1
  129.2 5.4 %copy.172 = f32[16,4,32,128]{2,0,1,3:T(8,128)} copy(f32[16,4,32,128]{3,2,1,0:T(8,128)} %bitcast.442) | data formatting | bytes 2097152 | tf_op jit(solution)/shard_map/reshape.7
  134.6 8.1 %fusion.17 = f32[128,4,32,16]{2,3,1,0:T(8,128)} fusion(f32[16,4,32,128]{2,0,1,3:T(8,128)} %copy.172, f32[16,128]{0,1:T(8,128)S(1)} %copy.167, pred[16,16]{0,1:T(8,128)(4,1)S(1)} %iota_compare_fusion.2), kind=kOutput, calls=%fused_computation.72 | convolution fusion | flops 50429952 | bytes 2105600 | tf_op jit(solution)/shard_map/tkp,strcp->skrcp/dot_general | solution.py:111
  142.8 4.5 %copy.173 = f32[128,4,32,16]{0,2,1,3:T(8,128)} copy(f32[128,4,32,16]{2,3,1,0:T(8,128)} %fusion.17) | data formatting | bytes 2097152 | tf_op jit(solution)/shard_map/tkp,strcp->skrcp/dot_general | solution.py:111
  148.2 5.1 %all_gather.11 = bf16[2,1,4,32,128]{4,3,2,1,0:T(8,128)(2,1)S(1)} all-gather(bf16[1,1,4,32,128]{4,3,2,1,0:T(8,128)(2,1)S(1)} %fusion.71), channel_id=1, replica_groups=mesh['tm'=2,'rows'=4,'dp'=4] {'tm'}, dimensions={0}, use_global_device_ids=true | all-gather | bytes 98304 | tf_op jit(solution)/shard_map/all_gather | solution.py:115
  153.3 1.9 fusion.16
  155.9 1.0 convolution_bitcast_fusion.14
  157.6 1.0 convolution_bitcast_fusion.11
  158.6 1.0 convolution_bitcast_fusion.9
  159.5 1.0 convolution_bitcast_fusion.17
  160.5 1.0 convolution_bitcast_fusion.15
  161.6 57.8 %psum.31 = f32[16,128]{0,1:T(8,128)S(1)} all-reduce(f32[16,128]{0,1:T(8,128)S(1)} %copy.212), channel_id=1, replica_groups=mesh['tm'=2,'rows'=4,'dp'=4] {'rows','dp'}, use_global_device_ids=true, to_apply=%region_7.8 | all-reduce | flops 2048 | bytes 16384 | tf_op jit(solution)/shard_map/psum | solution.py:133
  219.4 1.3 collective-permute-start.6
  220.7 1.3 collective-permute-start.7
  225.4 2.2 collective-permute-done.7
  231.8 1.0 add_convert_fusion
  232.8 124.3 %all-reduce.7.cloned.1.call-done = (f32[3,3,128,128]{3,2,1,0:T(8,128)}, f32[3,3,128,128]{3,2,1,0:T(8,128)}) async-done(((f32[3,3,128,128]{3,2,1,0:T(8,128)}, f32[3,3,128,128]{3,2,1,0:T(8,128)}), (f32[3,3,128,128]{3,2,1,0:T(8,128)}, f32[3,3,128,128]{3,2,1,0:T(8,128)})) %all-reduce.7.cloned.1.call-update) | async-done | bytes 1179664 | tf_op jit(solution)/shard_map/psum | solution.py:138
  357.2 1.9 broadcast_multiply_fusion.1
  359.1 1.9 broadcast_multiply_fusion
  (110 shorter events, 26.8 us)
Async XLA Ops:
  7.2 350.0 %all-reduce.7.cloned.1.call-start = ((), (), s32[]{:S(2)}) async-start(), calls=%async_computation | async-start | bytes 2359296 | tf_op jit(solution)/shard_map/psum | solution.py:138
  8.2 11.5 %collective-permute-start = (bf16[1,16,1,32,128]{4,3,2,1,0:T(8,128)(2,1)S(1)}, bf16[1,16,1,32,128]{4,3,2,1,0:T(8,128)(2,1)S(1)}, u32[]{:S(2)}, u32[]{:S(2)}) collective-permute-start(bf16[1,16,1,32,128]{4,3,2,1,0:T(8,128)(2,1)S(1)} %get-tuple-element.71), channel_id=1, source_target_pairs={{0,4},{4,8},{8,12},{1,5},{5,9},{9,13},{2,6},{6,10},{10,14},{3,7},{... | collective-permute-start | bytes 393224 | tf_op jit(solution)/shard_map/ppermute | solution.py:16
  13.2 6.9 %collective-permute-start.1 = (bf16[1,16,1,32,128]{4,3,2,1,0:T(8,128)(2,1)S(1)}, bf16[1,16,1,32,128]{4,3,2,1,0:T(8,128)(2,1)S(1)}, u32[]{:S(2)}, u32[]{:S(2)}) collective-permute-start(bf16[1,16,1,32,128]{4,3,2,1,0:T(8,128)(2,1)S(1)} %get-tuple-element.72), channel_id=1, source_target_pairs={{4,0},{8,4},{12,8},{5,1},{9,5},{13,9},{6,2},{10,6},{14,10},{7,3},{... | collective-permute-start | bytes 393224 | tf_op jit(solution)/shard_map/ppermute | solution.py:18
  21.7 1.0 copy-start.6
  22.3 1.1 copy-start
  23.4 0.8 copy-start.3
  23.4 1.9 copy-start.1
  42.1 10.6 %copy-start.10 = (f32[16,128]{1,0:T(8,128)S(1)}, f32[16,128]{1,0:T(8,128)}, u32[]{:S(2)}) copy-start(f32[16,128]{1,0:T(8,128)} %param.11) | copy-start | bytes 24580
  47.0 6.9 %collective-permute-start.2 = (bf16[1,16,1,32,128]{4,3,2,1,0:T(8,128)(2,1)S(1)}, bf16[1,16,1,32,128]{4,3,2,1,0:T(8,128)(2,1)S(1)}, u32[]{:S(2)}, u32[]{:S(2)}) collective-permute-start(bf16[1,16,1,32,128]{4,3,2,1,0:T(8,128)(2,1)S(1)} %get-tuple-element.67), channel_id=1, source_target_pairs={{0,4},{4,8},{8,12},{1,5},{5,9},{9,13},{2,6},{6,10},{10,14},{3,7},{... | collective-permute-start | bytes 393224 | tf_op jit(solution)/shard_map/ppermute | solution.py:16
  51.2 6.9 %collective-permute-start.3 = (bf16[1,16,1,32,128]{4,3,2,1,0:T(8,128)(2,1)S(1)}, bf16[1,16,1,32,128]{4,3,2,1,0:T(8,128)(2,1)S(1)}, u32[]{:S(2)}, u32[]{:S(2)}) collective-permute-start(bf16[1,16,1,32,128]{4,3,2,1,0:T(8,128)(2,1)S(1)} %get-tuple-element.68), channel_id=1, source_target_pairs={{4,0},{8,4},{12,8},{5,1},{9,5},{13,9},{6,2},{10,6},{14,10},{7,3},{... | collective-permute-start | bytes 393224 | tf_op jit(solution)/shard_map/ppermute | solution.py:18
  58.6 1.0 copy-start.5
  61.9 1.0 copy-start.8
  61.9 1.0 copy-start.11
  115.1 7.3 %collective-permute-start.4 = (bf16[1,16,1,32,128]{4,3,2,1,0:T(8,128)(2,1)}, bf16[1,16,1,32,128]{4,3,2,1,0:T(8,128)(2,1)S(1)}, u32[]{:S(2)}, u32[]{:S(2)}) collective-permute-start(bf16[1,16,1,32,128]{4,3,2,1,0:T(8,128)(2,1)} %get-tuple-element.63), channel_id=1, source_target_pairs={{0,4},{4,8},{8,12},{1,5},{5,9},{9,13},{2,6},{6,10},{10,14},{3,7},{... | collective-permute-start | bytes 393224 | tf_op jit(solution)/shard_map/ppermute | solution.py:16
  117.3 7.1 %collective-permute-start.5 = (bf16[1,16,1,32,128]{4,3,2,1,0:T(8,128)(2,1)}, bf16[1,16,1,32,128]{4,3,2,1,0:T(8,128)(2,1)S(1)}, u32[]{:S(2)}, u32[]{:S(2)}) collective-permute-start(bf16[1,16,1,32,128]{4,3,2,1,0:T(8,128)(2,1)} %get-tuple-element.64), channel_id=1, source_target_pairs={{4,0},{8,4},{12,8},{5,1},{9,5},{13,9},{6,2},{10,6},{14,10},{7,3},{... | collective-permute-start | bytes 393224 | tf_op jit(solution)/shard_map/ppermute | solution.py:18
  147.3 7.9 %copy-start.2 = (bf16[1,16,4,32,128]{4,3,2,1,0:T(8,128)(2,1)S(1)}, bf16[1,16,4,32,128]{4,3,2,1,0:T(8,128)(2,1)}, u32[]{:S(2)}) copy-start(bf16[1,16,4,32,128]{4,3,2,1,0:T(8,128)(2,1)} %copy-done.1) | copy-start | bytes 1572868
  153.3 2.3 copy-start.4
  160.5 61.5 %copy-start.9 = (f32[1,128,128]{2,1,0:T(8,128)S(1)}, f32[1,128,128]{2,1,0:T(8,128)}, u32[]{:S(2)}) copy-start(f32[1,128,128]{2,1,0:T(8,128)} %convolution_bitcast_fusion.14) | copy-start | bytes 196612
  219.4 6.0 %collective-permute-start.6 = (bf16[1,16,1,32,128]{4,3,2,1,0:T(8,128)(2,1)S(1)}, bf16[1,16,1,32,128]{4,3,2,1,0:T(8,128)(2,1)S(1)}, u32[]{:S(2)}, u32[]{:S(2)}) collective-permute-start(bf16[1,16,1,32,128]{4,3,2,1,0:T(8,128)(2,1)S(1)} %get-tuple-element.59), channel_id=1, source_target_pairs={{0,4},{4,8},{8,12},{1,5},{5,9},{9,13},{2,6},{6,10},{10,14},{3,7},{... | collective-permute-start | bytes 393224 | tf_op jit(solution)/shard_map/ppermute | solution.py:16
  220.7 6.9 %collective-permute-start.7 = (bf16[1,16,1,32,128]{4,3,2,1,0:T(8,128)(2,1)S(1)}, bf16[1,16,1,32,128]{4,3,2,1,0:T(8,128)(2,1)S(1)}, u32[]{:S(2)}, u32[]{:S(2)}) collective-permute-start(bf16[1,16,1,32,128]{4,3,2,1,0:T(8,128)(2,1)S(1)} %get-tuple-element.60), channel_id=1, source_target_pairs={{4,0},{8,4},{12,8},{5,1},{9,5},{13,9},{6,2},{10,6},{14,10},{7,3},{... | collective-permute-start | bytes 393224 | tf_op jit(solution)/shard_map/ppermute | solution.py:18
  228.0 1.0 copy-start.7
Sparse Core Ops, SparseCore 0:
  225.5 131.6 all-reduce.6
where the time goes:
time: 369 us; the launch traced here: 368 us
  waiting for transfers between devices  133 us (36%)
  blocking collectives  112 us (30%)
  matrix products  42.6 us (12%)
  local copies, waits for them, and re-layouts  26.5 us (7%)
  other arithmetic  20.8 us (6%)
  starting transfers between devices  18.3 us (5%)
  between operations  14.6 us (4%)
    psum x1, waiting for transfers between devices, on_device(): lax.psum((in_grad, out_grad, gain_grad), ('tm', 'rows', 'dp'))  124 us
    psum x1, blocking collectives, on_device(): decay_grad = lax.psum(decay_part, ('rows', 'dp')) * decay_scale  57.8 us
    psum x1, blocking collectives, on_device(): lax.psum((in_grad, out_grad, gain_grad), ('tm', 'rows', 'dp'))  40.4 us
    dot_general x18, matrix products, kernel_grad(): lax.dot_general(piece, flat_grad, (((0,), (0,)), ((), ())), preferred_ele...  14.9 us
    ppermute x4, starting transfers between devices, padded_2(): lax.ppermute(tail, axis, [(i, (i + 1) % count) for i in range(ends)])  12.7 us
    ppermute x4, waiting for transfers between devices, padded_2(): lax.ppermute(head, axis, [((i + 1) % count, i) for i in range(ends)])  8.64 us
    dot_general x1, matrix products, on_device(): jnp.einsum('tkp,skrcp->strcp', within, drive, precision=lax.Precision.HIG...  8.27 us
    dot_general x1, matrix products, on_device(): jnp.einsum('tkp,strcp->skrcp', within, state_grad, precision=lax.Precisio...  8.14 us
  transfers between devices with their start and end apart: 9, of which 5 were waited for; matrix products, arithmetic and copies ran while one was open for 4% of the time, Pallas kernels for 0%

commit v1 on v0

--- a/solution.py
+++ b/solution.py
@@ -135,7 +135,9 @@
     in_grad = kernel_grad(padded_x, adjoint_bf)
     padded_a = pad_columns(padded_2(adjoint_bf, (("rows", 2),), 1))
     video_grad = (adjoint_conv(padded_a, in_kernel) + skip_gain * grad_pre).astype(jnp.bfloat16)
-    in_sum, out_sum, gain_sum = lax.psum((in_grad, out_grad, gain_grad), ("tm", "rows", "dp"))
+    in_sum, out_sum, gain_sum = lax.psum(
+        lax.psum((in_grad, out_grad, gain_grad), axis_name=("rows", "dp")), axis_name="tm"
+    )
     weight_scale = 1.0 / math.sqrt(
         seqs
         * frames

time: 369 us -> 337 us (0.913)
  blocking collectives: 112 us -> 76.9 us
    psum x2, blocking collectives: 98.2 us -> 63.3 us  [the longest x1 58.3 us: on_device(): lax.psum((in_grad, out_grad, gain_grad), axis_name=('rows', 'dp'))]
    dot_general x18, matrix products: 14.9 us -> 11.1 us  [kernel_grad(): lax.dot_general(piece, flat_grad, (((0,), (0,)), ((), ())), preferred_ele...]
    psum x1 -> x2, waiting for transfers between devices: 124 us -> 125 us  [the longest x1 84.8 us: on_device(): lax.psum((in_grad, out_grad, gain_grad), axis_name=('rows', 'dp'))]
  transfers between devices with their start and end apart: 9 -> 10, of which waited for: 5 -> 6; matrix products, arithmetic and copies ran while one was open for 4% -> 5% of each run, Pallas kernels for 0% -> 0%
where the time goes in v1:
time: 337 us; the launch traced here: 336 us
  waiting for transfers between devices  136 us (40%)
  blocking collectives  76.9 us (23%)
  matrix products  42.2 us (13%)
  local copies, waits for them, and re-layouts  27.8 us (8%)
  starting transfers between devices  19.6 us (6%)
  other arithmetic  18.2 us (5%)
  between operations  14.7 us (4%)
    psum x1, waiting for transfers between devices, on_device(): lax.psum((in_grad, out_grad, gain_grad), axis_name=('rows', 'dp'))  84.8 us
    psum x1, blocking collectives, on_device(): lax.psum((in_grad, out_grad, gain_grad), axis_name=('rows', 'dp'))  58.3 us
    psum x1, waiting for transfers between devices, on_device(): lax.psum(lax.psum((in_grad, out_grad, gain_grad), axis_name=('rows', 'dp'...  40.2 us
    ppermute x4, starting transfers between devices, padded_2(): lax.ppermute(tail, axis, [(i, (i + 1) % count) for i in range(ends)])  14 us
    dot_general x18, matrix products, kernel_grad(): lax.dot_general(piece, flat_grad, (((0,), (0,)), ((), ())), preferred_ele...  11.1 us
    ppermute x4, waiting for transfers between devices, padded_2(): lax.ppermute(head, axis, [((i + 1) % count, i) for i in range(ends)])  11.1 us
    dot_general x18, matrix products, adjoint_conv(): lax.dot_general(piece, kernel[i, j], (((1,), (1,)), ((), ())), preferred_...  9.56 us
    dot_general x1, matrix products, on_device(): jnp.einsum('tkp,skrcp->strcp', within, drive, precision=lax.Precision.HIG...  8.31 us
  transfers between devices with their start and end apart: 10, of which 6 were waited for; matrix products, arithmetic and copies ran while one was open for 5% of the time, Pallas kernels for 0%

profile of v1, /device:TPU:0, one launch (start us, length us, event | category | flops | bytes accessed | tf_op | source)
XLA Modules:
  0.0 335.6 jit_solution(17731125966195582412)
XLA Ops:
  7.2 1.0 fusion.177
  8.2 5.0 %collective-permute-start = (bf16[1,16,1,32,128]{4,3,2,1,0:T(8,128)(2,1)S(1)}, bf16[1,16,1,32,128]{4,3,2,1,0:T(8,128)(2,1)S(1)}, u32[]{:S(2)}, u32[]{:S(2)}) collective-permute-start(bf16[1,16,1,32,128]{4,3,2,1,0:T(8,128)(2,1)S(1)} %get-tuple-element.75), channel_id=1, source_target_pairs={{0,4},{4,8},{8,12},{1,5},{5,9},{9,13},{2,6},{6,10},{10,14},{3,7},{... | collective-permute-start | bytes 393224 | tf_op jit(solution)/shard_map/ppermute | solution.py:16
  13.2 1.3 collective-permute-start.1
  15.2 4.2 %all-gather = f32[2,1,128]{2,1,0:T(1,128)S(1)} all-gather(f32[1,1,128]{2,1,0:T(1,128)S(1)} %slice_bitcast_fusion.1), channel_id=1, replica_groups=mesh['tm'=2,'rows'=4,'dp'=4] {'tm'}, dimensions={0}, use_global_device_ids=true | all-gather | bytes 1536 | tf_op jit(solution)/shard_map/all_gather | solution.py:87
  20.0 1.6 fusion.25
  25.6 4.5 %copy.169 = f32[16,4,32,128]{2,0,1,3:T(8,128)} copy(f32[16,4,32,128]{3,2,1,0:T(8,128)S(1)} %bitcast.443) | data formatting | bytes 2097152 | tf_op jit(solution)/shard_map/reshape
  30.1 8.3 %fusion.19 = f32[128,4,32,16]{2,3,1,0:T(8,128)} fusion(f32[16,4,32,128]{2,0,1,3:T(8,128)} %copy.169, f32[16,128]{0,1:T(8,128)S(1)} %copy.167, pred[16,16]{0,1:T(8,128)(4,1)S(1)} %iota_compare_fusion.2), kind=kOutput, calls=%fused_computation.74 | convolution fusion | flops 50429952 | bytes 2105600 | tf_op jit(solution)/shard_map/tkp,skrcp->strcp/dot_general | solution.py:84
  38.4 3.7 %copy.171 = f32[128,4,32,16]{0,2,1,3:T(8,128)S(1)} copy(f32[128,4,32,16]{2,3,1,0:T(8,128)} %fusion.19) | data formatting | bytes 2097152 | tf_op jit(solution)/shard_map/tkp,skrcp->strcp/dot_general | solution.py:84
  42.2 4.6 %all_gather.9 = bf16[2,1,4,32,128]{4,3,2,1,0:T(8,128)(2,1)S(1)} all-gather(bf16[1,1,4,32,128]{4,3,2,1,0:T(8,128)(2,1)S(1)} %slice.550), channel_id=1, replica_groups=mesh['tm'=2,'rows'=4,'dp'=4] {'tm'}, dimensions={0}, use_global_device_ids=true | all-gather | bytes 98304 | tf_op jit(solution)/shard_map/all_gather | solution.py:91
  47.0 4.2 %collective-permute-start.2 = (bf16[1,16,1,32,128]{4,3,2,1,0:T(8,128)(2,1)S(1)}, bf16[1,16,1,32,128]{4,3,2,1,0:T(8,128)(2,1)S(1)}, u32[]{:S(2)}, u32[]{:S(2)}) collective-permute-start(bf16[1,16,1,32,128]{4,3,2,1,0:T(8,128)(2,1)S(1)} %get-tuple-element.71), channel_id=1, source_target_pairs={{0,4},{4,8},{8,12},{1,5},{5,9},{9,13},{2,6},{6,10},{10,14},{3,7},{... | collective-permute-start | bytes 393224 | tf_op jit(solution)/shard_map/ppermute | solution.py:16
  51.2 1.5 collective-permute-start.3
  52.7 1.1 slice.347
  53.9 4.2 %collective-permute-done.3 = bf16[1,16,1,32,128]{4,3,2,1,0:T(8,128)(2,1)S(1)} collective-permute-done((bf16[1,16,1,32,128]{4,3,2,1,0:T(8,128)(2,1)S(1)}, bf16[1,16,1,32,128]{4,3,2,1,0:T(8,128)(2,1)S(1)}, u32[]{:S(2)}, u32[]{:S(2)}) %collective-permute-start.3) | collective-permute-done | bytes 131104 | tf_op jit(solution)/shard_map/ppermute | solution.py:18
  63.0 1.8 fusion.6
  68.0 3.5 %collective-permute-start.4 = (bf16[1,16,1,32,128]{4,3,2,1,0:T(8,128)(2,1)S(1)}, bf16[1,16,1,32,128]{4,3,2,1,0:T(8,128)(2,1)S(1)}, u32[]{:S(2)}, u32[]{:S(2)}) collective-permute-start(bf16[1,16,1,32,128]{4,3,2,1,0:T(8,128)(2,1)S(1)} %get-tuple-element.67), channel_id=1, source_target_pairs={{0,4},{4,8},{8,12},{1,5},{5,9},{9,13},{2,6},{6,10},{10,14},{3,7},{... | collective-permute-start | bytes 393224 | tf_op jit(solution)/shard_map/ppermute | solution.py:16
  71.5 1.5 collective-permute-start.5
  74.0 4.4 %collective-permute-done.5 = bf16[1,16,1,32,128]{4,3,2,1,0:T(8,128)(2,1)S(1)} collective-permute-done((bf16[1,16,1,32,128]{4,3,2,1,0:T(8,128)(2,1)S(1)}, bf16[1,16,1,32,128]{4,3,2,1,0:T(8,128)(2,1)S(1)}, u32[]{:S(2)}, u32[]{:S(2)}) %collective-permute-start.5) | collective-permute-done | bytes 131104 | tf_op jit(solution)/shard_map/ppermute | solution.py:18
  82.0 1.3 fusion.1
  83.3 5.4 %copy.172 = f32[16,4,32,128]{2,0,1,3:T(8,128)} copy(f32[16,4,32,128]{3,2,1,0:T(8,128)} %bitcast.442) | data formatting | bytes 2097152 | tf_op jit(solution)/shard_map/reshape.7
  88.7 8.2 %fusion.17 = f32[128,4,32,16]{2,3,1,0:T(8,128)} fusion(f32[16,4,32,128]{2,0,1,3:T(8,128)} %copy.172, f32[16,128]{0,1:T(8,128)S(1)} %copy.167, pred[16,16]{0,1:T(8,128)(4,1)S(1)} %iota_compare_fusion.2), kind=kOutput, calls=%fused_computation.72 | convolution fusion | flops 50429952 | bytes 2105600 | tf_op jit(solution)/shard_map/tkp,strcp->skrcp/dot_general | solution.py:111
  96.9 4.5 %copy.173 = f32[128,4,32,16]{0,2,1,3:T(8,128)} copy(f32[128,4,32,16]{2,3,1,0:T(8,128)} %fusion.17) | data formatting | bytes 2097152 | tf_op jit(solution)/shard_map/tkp,strcp->skrcp/dot_general | solution.py:111
  101.4 0.9 fusion.71
  102.3 4.8 %all_gather.11 = bf16[2,1,4,32,128]{4,3,2,1,0:T(8,128)(2,1)S(1)} all-gather(bf16[1,1,4,32,128]{4,3,2,1,0:T(8,128)(2,1)S(1)} %fusion.71), channel_id=1, replica_groups=mesh['tm'=2,'rows'=4,'dp'=4] {'tm'}, dimensions={0}, use_global_device_ids=true | all-gather | bytes 98304 | tf_op jit(solution)/shard_map/all_gather | solution.py:115
  107.2 1.9 fusion.16
  109.0 1.0 convolution_bitcast_fusion.10
  110.0 1.0 convolution_bitcast_fusion.16
  111.0 1.0 convolution_bitcast_fusion.14
  111.9 1.0 convolution_bitcast_fusion.13
  113.2 1.0 convolution_bitcast_fusion.11
  114.2 1.0 convolution_bitcast_fusion.9
  115.2 1.0 convolution_bitcast_fusion.17
  116.2 1.0 convolution_bitcast_fusion.15
  117.2 58.3 %all-reduce.4 = (f32[128]{0:T(128)S(1)}, f32[16,128]{0,1:T(8,128)S(1)}) all-reduce(f32[128]{0:T(128)S(1)} %get-tuple-element.30, f32[16,128]{0,1:T(8,128)S(1)} %copy.212), channel_id=1, replica_groups=mesh['tm'=2,'rows'=4,'dp'=4] {'rows','dp'}, use_global_device_ids=true, to_apply=%region_7.8 | all-reduce | flops 2176 | bytes 17408 | tf_op jit(solution)/shard_map/psum | solution.py:139
  175.6 4.9 %psum.54 = f32[128]{0:T(128)S(1)} all-reduce(f32[128]{0:T(128)S(1)} %get-tuple-element.24), channel_id=1, replica_groups=mesh['tm'=2,'rows'=4,'dp'=4] {'tm'}, use_global_device_ids=true, to_apply=%region_8.9 | all-reduce | flops 128 | bytes 1024 | tf_op jit(solution)/shard_map/psum | solution.py:138
  181.2 1.3 collective-permute-start.6
  182.5 1.3 collective-permute-start.7
  183.8 0.9 maximum_bitcast_fusion.2
  184.7 0.9 maximum_bitcast_fusion
  187.1 2.2 collective-permute-done.7
  190.5 1.4 fusion.170
  192.9 1.3 fusion.94
  194.5 1.3 convolution_add_fusion.3
  195.8 84.8 %all-reduce.10.cloned.1.call-done = (f32[3,3,128,128]{3,2,1,0:T(8,128)}, f32[3,3,128,128]{3,2,1,0:T(8,128)}) async-done(((f32[3,3,128,128]{3,2,1,0:T(8,128)}, f32[3,3,128,128]{3,2,1,0:T(8,128)}), (f32[3,3,128,128]{3,2,1,0:T(8,128)}, f32[3,3,128,128]{3,2,1,0:T(8,128)})) %all-reduce.10.cloned.1.call-update) | async-done | bytes 1179664 | tf_op jit(solution)/shard_map/psum | solution.py:139
  280.6 1.5 convolution_add_fusion.2
  283.6 1.0 add_convert_fusion
  284.7 40.2 %all-reduce.12.cloned.1.call-done = (f32[3,3,128,128]{3,2,1,0:T(8,128)}, f32[3,3,128,128]{3,2,1,0:T(8,128)}) async-done(((f32[3,3,128,128]{3,2,1,0:T(8,128)}, f32[3,3,128,128]{3,2,1,0:T(8,128)}), (f32[3,3,128,128]{3,2,1,0:T(8,128)}, f32[3,3,128,128]{3,2,1,0:T(8,128)})) %all-reduce.12.cloned.1.call-update) | async-done | bytes 1179664 | tf_op jit(solution)/shard_map/psum | solution.py:138
  324.9 1.9 broadcast_multiply_fusion.1
  326.8 1.9 broadcast_multiply_fusion
  (123 shorter events, 24.5 us)
Async XLA Ops:
  7.2 273.4 %all-reduce.10.cloned.1.call-start = ((), (), s32[]{:S(2)}) async-start(), calls=%async_computation | async-start | bytes 2359296 | tf_op jit(solution)/shard_map/psum | solution.py:139
  8.2 11.5 %collective-permute-start = (bf16[1,16,1,32,128]{4,3,2,1,0:T(8,128)(2,1)S(1)}, bf16[1,16,1,32,128]{4,3,2,1,0:T(8,128)(2,1)S(1)}, u32[]{:S(2)}, u32[]{:S(2)}) collective-permute-start(bf16[1,16,1,32,128]{4,3,2,1,0:T(8,128)(2,1)S(1)} %get-tuple-element.75), channel_id=1, source_target_pairs={{0,4},{4,8},{8,12},{1,5},{5,9},{9,13},{2,6},{6,10},{10,14},{3,7},{... | collective-permute-start | bytes 393224 | tf_op jit(solution)/shard_map/ppermute | solution.py:16
  13.2 6.9 %collective-permute-start.1 = (bf16[1,16,1,32,128]{4,3,2,1,0:T(8,128)(2,1)S(1)}, bf16[1,16,1,32,128]{4,3,2,1,0:T(8,128)(2,1)S(1)}, u32[]{:S(2)}, u32[]{:S(2)}) collective-permute-start(bf16[1,16,1,32,128]{4,3,2,1,0:T(8,128)(2,1)S(1)} %get-tuple-element.76), channel_id=1, source_target_pairs={{4,0},{8,4},{12,8},{5,1},{9,5},{13,9},{6,2},{10,6},{14,10},{7,3},{... | collective-permute-start | bytes 393224 | tf_op jit(solution)/shard_map/ppermute | solution.py:18
  21.7 1.0 copy-start.9
  22.3 1.1 copy-start
  23.4 0.8 copy-start.4
  23.4 1.9 copy-start.2
  42.1 10.6 %copy-start.15 = (f32[16,128]{1,0:T(8,128)S(1)}, f32[16,128]{1,0:T(8,128)}, u32[]{:S(2)}) copy-start(f32[16,128]{1,0:T(8,128)} %param.11) | copy-start | bytes 24580
  47.0 6.9 %collective-permute-start.2 = (bf16[1,16,1,32,128]{4,3,2,1,0:T(8,128)(2,1)S(1)}, bf16[1,16,1,32,128]{4,3,2,1,0:T(8,128)(2,1)S(1)}, u32[]{:S(2)}, u32[]{:S(2)}) collective-permute-start(bf16[1,16,1,32,128]{4,3,2,1,0:T(8,128)(2,1)S(1)} %get-tuple-element.71), channel_id=1, source_target_pairs={{0,4},{4,8},{8,12},{1,5},{5,9},{9,13},{2,6},{6,10},{10,14},{3,7},{... | collective-permute-start | bytes 393224 | tf_op jit(solution)/shard_map/ppermute | solution.py:16
  51.2 6.9 %collective-permute-start.3 = (bf16[1,16,1,32,128]{4,3,2,1,0:T(8,128)(2,1)S(1)}, bf16[1,16,1,32,128]{4,3,2,1,0:T(8,128)(2,1)S(1)}, u32[]{:S(2)}, u32[]{:S(2)}) collective-permute-start(bf16[1,16,1,32,128]{4,3,2,1,0:T(8,128)(2,1)S(1)} %get-tuple-element.72), channel_id=1, source_target_pairs={{4,0},{8,4},{12,8},{5,1},{9,5},{13,9},{6,2},{10,6},{14,10},{7,3},{... | collective-permute-start | bytes 393224 | tf_op jit(solution)/shard_map/ppermute | solution.py:18
  58.6 1.0 copy-start.8
  61.9 1.0 copy-start.12
  62.0 1.0 copy-start.16
  68.0 6.0 %collective-permute-start.4 = (bf16[1,16,1,32,128]{4,3,2,1,0:T(8,128)(2,1)S(1)}, bf16[1,16,1,32,128]{4,3,2,1,0:T(8,128)(2,1)S(1)}, u32[]{:S(2)}, u32[]{:S(2)}) collective-permute-start(bf16[1,16,1,32,128]{4,3,2,1,0:T(8,128)(2,1)S(1)} %get-tuple-element.67), channel_id=1, source_target_pairs={{0,4},{4,8},{8,12},{1,5},{5,9},{9,13},{2,6},{6,10},{10,14},{3,7},{... | collective-permute-start | bytes 393224 | tf_op jit(solution)/shard_map/ppermute | solution.py:16
  71.5 6.9 %collective-permute-start.5 = (bf16[1,16,1,32,128]{4,3,2,1,0:T(8,128)(2,1)S(1)}, bf16[1,16,1,32,128]{4,3,2,1,0:T(8,128)(2,1)S(1)}, u32[]{:S(2)}, u32[]{:S(2)}) collective-permute-start(bf16[1,16,1,32,128]{4,3,2,1,0:T(8,128)(2,1)S(1)} %get-tuple-element.68), channel_id=1, source_target_pairs={{4,0},{8,4},{12,8},{5,1},{9,5},{13,9},{6,2},{10,6},{14,10},{7,3},{... | collective-permute-start | bytes 393224 | tf_op jit(solution)/shard_map/ppermute | solution.py:18
  101.4 7.6 %copy-start.3 = (bf16[1,16,4,32,128]{4,3,2,1,0:T(8,128)(2,1)S(1)}, bf16[1,16,4,32,128]{4,3,2,1,0:T(8,128)(2,1)}, u32[]{:S(2)}) copy-start(bf16[1,16,4,32,128]{4,3,2,1,0:T(8,128)(2,1)} %copy-done.2) | copy-start | bytes 1572868
  107.1 2.9 copy-start.5
  116.1 67.6 %copy-start.13 = (f32[1,128,128]{2,1,0:T(8,128)S(1)}, f32[1,128,128]{2,1,0:T(8,128)}, u32[]{:S(2)}) copy-start(f32[1,128,128]{2,1,0:T(8,128)} %convolution_bitcast_fusion.13) | copy-start | bytes 196612
  116.2 67.6 %copy-start.14 = (f32[1,128,128]{2,1,0:T(8,128)S(1)}, f32[1,128,128]{2,1,0:T(8,128)}, u32[]{:S(2)}) copy-start(f32[1,128,128]{2,1,0:T(8,128)} %convolution_bitcast_fusion.14) | copy-start | bytes 196612
  181.2 5.9 %collective-permute-start.6 = (bf16[1,16,1,32,128]{4,3,2,1,0:T(8,128)(2,1)S(1)}, bf16[1,16,1,32,128]{4,3,2,1,0:T(8,128)(2,1)S(1)}, u32[]{:S(2)}, u32[]{:S(2)}) collective-permute-start(bf16[1,16,1,32,128]{4,3,2,1,0:T(8,128)(2,1)S(1)} %get-tuple-element.63), channel_id=1, source_target_pairs={{0,4},{4,8},{8,12},{1,5},{5,9},{9,13},{2,6},{6,10},{10,14},{3,7},{... | collective-permute-start | bytes 393224 | tf_op jit(solution)/shard_map/ppermute | solution.py:16
  182.5 6.9 %collective-permute-start.7 = (bf16[1,16,1,32,128]{4,3,2,1,0:T(8,128)(2,1)S(1)}, bf16[1,16,1,32,128]{4,3,2,1,0:T(8,128)(2,1)S(1)}, u32[]{:S(2)}, u32[]{:S(2)}) collective-permute-start(bf16[1,16,1,32,128]{4,3,2,1,0:T(8,128)(2,1)S(1)} %get-tuple-element.64), channel_id=1, source_target_pairs={{4,0},{8,4},{12,8},{5,1},{9,5},{13,9},{6,2},{10,6},{14,10},{7,3},{... | collective-permute-start | bytes 393224 | tf_op jit(solution)/shard_map/ppermute | solution.py:18
  186.5 138.4 %all-reduce.12.cloned.1.call-start = ((), (), s32[]{:S(2)}) async-start(), calls=%async_computation.1 | async-start | bytes 2359296 | tf_op jit(solution)/shard_map/psum | solution.py:138
  189.3 0.6 copy-start.10
  190.5 1.7 copy-start.11
  194.5 86.1 %copy-start.7 = (bf16[1,16,4,32,128]{4,3,2,1,0:T(8,128)(2,1)S(1)}, bf16[1,16,4,32,128]{4,3,2,1,0:T(8,128)(2,1)}, u32[]{:S(2)}) copy-start(bf16[1,16,4,32,128]{4,3,2,1,0:T(8,128)(2,1)} %get-tuple-element.38) | copy-start | bytes 1572868
  195.8 86.3 %copy-start.6 = (bf16[1,16,4,32,128]{4,3,2,1,0:T(8,128)(2,1)S(1)}, bf16[1,16,4,32,128]{4,3,2,1,0:T(8,128)(2,1)}, u32[]{:S(2)}) copy-start(bf16[1,16,4,32,128]{4,3,2,1,0:T(8,128)(2,1)} %get-tuple-element.37) | copy-start | bytes 1572868
  282.1 1.2 copy-start.1
Sparse Core Ops, SparseCore 0:
  186.7 93.8 all-reduce.9
  282.9 41.9 all-reduce.11
